TPU v7x, 256 devices: a whole 4x4x8 slice. The times are simulated.
256 devices in a mesh: tm: 16 (over y_lo, x, core), blk: 8 (over z), samp: 2 (over y_hi).
Axes of the slice: x: 4, y: 4 (y_hi: 2, y_lo: 2; y = y_hi * 2 + y_lo), z: 8, core: 2. Of those that a mesh axis runs over, the one named last changes fastest.
Arguments:
- prior_path: float32 [32, 16, 1024], P('tm', 'samp', 'blk'), may hold values from -6 to 6
- observed: float32 [32, 256], P('tm', 'blk'), may hold values from -6 to 6
- obs_mask: int32 [32, 32], P('tm', 'blk'), may hold values 0 or 1
- noise_draw: float32 [32, 16, 256], P('tm', 'samp', 'blk'), may hold values from -6 to 6
- wend_blocks: float32 [128, 8, 8], P('blk'), may hold values from -1 to 1
- block_cols: int32 [128], P('blk'), may hold values from 0 to 31, as said below
- start_mean: float32 [16, 1024], P('samp', 'blk'), may hold values from -6 to 6
- trans_mats: bfloat16 [32, 1024, 1024], P('tm', 'blk', 'samp')
- gain_mats: bfloat16 [32, 1024, 256], P('tm', 'blk', 'samp'), may hold values from -0.375 to 0.375
- smooth_mats: bfloat16 [32, 1024, 1024], P('tm', 'blk', 'samp')
- site_trans: float32 [4, 4], replicated, may hold values from -2.5 to 2.5
Outputs:
- posterior_path: float32 [32, 16, 1024], P('tm', 'samp', 'blk')
Inputs may be any that keep to these rules, and one draw needn't show every extreme that they name: `block_cols`: entry 4 i names block i itself, entries 4 i + 1 to 4 i + 3 name three different blocks among i - 2, i - 1, i + 1, i + 2 taken modulo 32.
All inputs are finite; a program needn't handle non-finite values. No bound on the sum of `obs_mask` on one device may be relied on, other than what follows from the above.
Results may differ from a plain program's by a relative error of at most 0.0003.
Values may be sent and summed in bfloat16 or wider, within the bound.
No kernel may reach another device: no remote copies, remote signals or barrier semaphores. Data moves between devices by JAX's collectives and lax.ppermute only.
A program may use at most 64 MiB of HBM per device.

v0:
```python
import jax
import jax.numpy as jnp
from jax import lax
from jax.sharding import PartitionSpec as P

highest = lax.Precision.HIGHEST


def with_halo(value, sides, width):
    for axis, dim in sides:
        count, length = (lax.axis_size(axis), value.shape[dim])
        up = [(i, (i + 1) % count) for i in range(count)]
        down = [(j, i) for i, j in up]
        last = lax.slice_in_dim(value, length - width, length, axis=dim)
        initial = lax.slice_in_dim(value, 0, width, axis=dim)
        before = lax.ppermute(last, axis, up)
        after = lax.ppermute(initial, axis, down)
        value = jnp.concatenate([before, value, after], axis=dim)
    return value


def shifted(value, axis, steps):
    count = lax.axis_size(axis)
    initial, last = (max(0, -steps), min(count, count - steps))
    return lax.ppermute(value, axis, [(source, source + steps) for source in range(initial, last)])


def apply_rows(matrix, states):
    return jnp.einsum("ij,sj->si", matrix, states, precision=highest)


def on_device(
    prior_path,
    observed,
    obs_mask,
    noise_draw,
    wend_blocks,
    block_cols,
    start_mean,
    trans_mats,
    gain_mats,
    smooth_mats,
    site_trans,
):
    trans_mats, gain_mats, smooth_mats = (
        lax.all_gather(trans_mats, "samp", axis=2, tiled=True),
        lax.all_gather(gain_mats, "samp", axis=2, tiled=True),
        lax.all_gather(smooth_mats, "samp", axis=2, tiled=True),
    )
    step_count, sample_count, local_sites = noise_draw.shape
    block_sites = wend_blocks.shape[1]
    local_blocks = local_sites // block_sites
    cycle_size = lax.axis_size("blk")
    block_count = local_blocks * cycle_size
    row_count = trans_mats.shape[1]
    state_count = row_count * cycle_size
    widened = with_halo(noise_draw, (("blk", 2),), 2 * block_sites)
    rim_blocks = widened.reshape(step_count, sample_count, local_blocks + 4, block_sites)
    pair_rows = jnp.arange(local_blocks * 4, dtype=jnp.int32) // 4
    first_block = lax.axis_index("blk") * local_blocks
    offset = (block_cols - first_block - pair_rows + 2) % block_count
    position = pair_rows + offset
    chooser = (position[:, None] == jnp.arange(local_blocks + 4, dtype=jnp.int32)[None, :]).astype(
        jnp.float32
    )
    picked = jnp.einsum("pl,tslj->tspj", chooser, rim_blocks, precision=highest)
    mixed = jnp.einsum("tspj,pij->tspi", picked, wend_blocks, precision=highest)
    obs_noise = jnp.sum(
        mixed.reshape(step_count, sample_count, local_blocks, 4, block_sites), axis=3
    ).reshape(step_count, sample_count, local_sites)
    first_comp = prior_path.reshape(step_count, sample_count, local_sites, 4)[:, :, :, 0]
    seen_mask = jnp.repeat(obs_mask.astype(jnp.float32), block_sites, axis=1)
    residual = seen_mask[:, None, :] * (observed[:, None, :] - first_comp - obs_noise)
    all_resid = lax.all_gather(residual, "blk", axis=2, tiled=True)
    inputs = jnp.einsum("tij,tsj->tsi", gain_mats, all_resid, precision=highest)
    left_trans = trans_mats[1]
    left_smooth = smooth_mats[0]
    forward_pair = jnp.dot(
        left_trans,
        lax.all_gather(trans_mats[0], "blk", axis=0, tiled=True),
        preferred_element_type=jnp.float32,
    )
    backward_pair = jnp.dot(
        left_smooth,
        lax.all_gather(smooth_mats[1], "blk", axis=0, tiled=True),
        preferred_element_type=jnp.float32,
    )
    first_input, initial = (
        lax.all_gather(inputs[0], "blk", axis=1, tiled=True),
        lax.all_gather(start_mean, "blk", axis=1, tiled=True),
    )
    carry_input = apply_rows(trans_mats[1], first_input) + inputs[1]
    is_first = lax.axis_index("tm") == 0
    time_size = lax.axis_size("tm")
    level_count = (time_size - 1).bit_length()
    matrix, vector = shifted((forward_pair, carry_input), "tm", 1)
    vector = jnp.where(is_first, start_mean, vector)
    for level in range(level_count):
        received_m, received_v = shifted((matrix, vector), "tm", 1 << level)
        complete_m, complete_v = (
            lax.all_gather(received_m, "blk", axis=0, tiled=True),
            lax.all_gather(received_v, "blk", axis=1, tiled=True),
        )
        matrix, vector = (
            jnp.dot(matrix, complete_m, precision=highest),
            apply_rows(matrix, complete_v) + vector,
        )
    entry_state = lax.all_gather(vector, "blk", axis=1, tiled=True)
    filtered = jnp.stack(
        [
            apply_rows(trans_mats[0], entry_state) + inputs[0],
            apply_rows(forward_pair, entry_state) + carry_input,
        ]
    )
    site_kron = jnp.kron(jnp.eye(row_count // 4, dtype=jnp.float32), site_trans)
    predicted = jnp.einsum("ij,tsj->tsi", site_kron, filtered, precision=highest)
    all_pred = lax.all_gather(predicted, "blk", axis=2, tiled=True)
    offsets = filtered - jnp.einsum("tij,tsj->tsi", smooth_mats, all_pred, precision=highest)
    is_last = lax.axis_index("tm") == time_size - 1
    late_offset = jnp.where(is_last, filtered[1], offsets[1])
    all_late = lax.all_gather(late_offset, "blk", axis=1, tiled=True)
    back_offset = apply_rows(smooth_mats[0], all_late) + offsets[0]

    def relay_back(relay_turn, later_now):
        emitted = apply_rows(backward_pair, later_now) + back_offset
        complete = lax.all_gather(emitted, "blk", axis=1, tiled=True)
        received = shifted(complete, "tm", -1)
        return jnp.where(lax.axis_index("tm") == time_size - 2 - relay_turn, received, later_now)

    later_state = lax.fori_loop(
        0, time_size - 1, relay_back, jnp.zeros((sample_count, state_count), jnp.float32)
    )
    smoothed = jnp.stack(
        [
            apply_rows(backward_pair, later_state) + back_offset,
            apply_rows(smooth_mats[1], later_state) + late_offset,
        ]
    )
    return prior_path + smoothed


def solution(mesh):
    placed = (
        P("tm", "samp", "blk"),
        P("tm", "blk"),
        P("tm", "blk"),
        P("tm", "samp", "blk"),
        P("blk", None, None),
        P("blk"),
        P("samp", "blk"),
        P("tm", "blk", "samp"),
        P("tm", "blk", "samp"),
        P("tm", "blk", "samp"),
        P(),
    )
    return jax.shard_map(
        on_device, mesh=mesh, in_specs=placed, out_specs=P("tm", "samp", "blk"), check_vma=False
    )
```

profile of v0, /device:TPU:7, one launch (start us, length us, event | category | flops | bytes accessed | tf_op | source)
XLA Modules:
  0.0 952.8 jit_solution(16144380244082695753)
XLA Ops:
  6.5 9.6 %all_gather.63 = bf16[2,128,1024]{2,1,0:T(8,128)(2,1)S(1)} all-gather(bf16[2,128,512]{2,1,0:T(8,128)(2,1)} %param.20), channel_id=1, replica_groups=mesh['tm'=16,'blk'=8,'samp'=2] {'samp'}, dimensions={2}, use_global_device_ids=true | all-gather | bytes 786432 | tf_op jit(solution)/shard_map/all_gather | solution.py:46
  16.9 41.3 %all-gather.17.cloned.1.call-done = bf16[1,1024,1024]{2,1,0:T(8,128)(2,1)} async-done(((bf16[1,128,1024]{2,1,0:T(8,128)(2,1)}), bf16[1,1024,1024]{2,1,0:T(8,128)(2,1)}) %all-gather.17.cloned.1.call-update) | async-done | bytes 2097168 | tf_op jit(solution)/shard_map/all_gather | solution.py:80
  58.2 2.0 fusion.4
  60.3 7.4 collective-permute-start.5
  67.6 6.1 collective-permute-done.5
  73.7 6.5 collective-permute-start.7
  80.2 6.1 collective-permute-done.7
  87.2 53.6 %all-gather.9.cloned.1.call-done = f32[1024,1024]{1,0:T(8,128)} async-done(((f32[128,1024]{1,0:T(8,128)}), f32[1024,1024]{1,0:T(8,128)}) %all-gather.9.cloned.1.call-update) | async-done | bytes 4194320 | tf_op jit(solution)/shard_map/all_gather | solution.py:101
  140.8 4.6 fusion.29
  145.5 3.2 collective-permute-start.9
  148.7 11.6 %collective-permute-done.9 = f32[128,1024]{1,0:T(8,128)S(1)} collective-permute-done((f32[128,1024]{1,0:T(8,128)S(1)}, f32[128,1024]{1,0:T(8,128)S(1)}, u32[]{:S(2)}, u32[]{:S(2)}) %collective-permute-start.9) | collective-permute-done | bytes 524320 | tf_op jit(solution)/shard_map/ppermute | solution.py:25
  161.2 8.4 all_gather.58
  170.5 45.1 %all-gather.11.cloned.1.call-done = f32[1024,1024]{1,0:T(8,128)} async-done(((f32[128,1024]{1,0:T(8,128)}), f32[1024,1024]{1,0:T(8,128)}) %all-gather.11.cloned.1.call-update) | async-done | bytes 4194320 | tf_op jit(solution)/shard_map/all_gather | solution.py:101
  215.6 4.6 fusion.30
  220.2 4.0 collective-permute-start.11
  224.2 12.2 %collective-permute-done.11 = f32[128,1024]{1,0:T(8,128)S(1)} collective-permute-done((f32[128,1024]{1,0:T(8,128)S(1)}, f32[128,1024]{1,0:T(8,128)S(1)}, u32[]{:S(2)}, u32[]{:S(2)}) %collective-permute-start.11) | collective-permute-done | bytes 524320 | tf_op jit(solution)/shard_map/ppermute | solution.py:25
  237.4 2.7 collective-permute-start.2
  240.1 5.4 all_gather.61
  246.9 19.8 %all_gather.60 = f32[2,8,256]{1,0,2:T(2,128)S(1)} all-gather(f32[2,8,32]{1,0,2:T(2,128)S(1)} %copy.27), channel_id=1, replica_groups=mesh['tm'=16,'blk'=8,'samp'=2] {'blk'}, dimensions={2}, use_global_device_ids=true | all-gather | bytes 18432 | tf_op jit(solution)/shard_map/all_gather | solution.py:74
  267.0 20.3 %all-gather.1 = f32[1,8,1024]{2,1,0:T(8,128)S(1)} all-gather(f32[1,8,128]{2,1,0:T(8,128)S(1)} %slice.52), channel_id=3, replica_groups=mesh['tm'=16,'blk'=8,'samp'=2] {'blk'}, dimensions={2}, use_global_device_ids=true | all-gather | bytes 36864 | tf_op jit(solution)/shard_map/all_gather | solution.py:89
  287.5 16.8 %collective-permute-start.3 = (f32[8,128]{1,0:T(8,128)S(1)}, f32[8,128]{1,0:T(8,128)S(1)}, u32[]{:S(2)}, u32[]{:S(2)}) collective-permute-start(f32[8,128]{1,0:T(8,128)S(1)} %convolution_add_fusion.4), channel_id=1, source_target_pairs={{0,16},{16,32},{32,48},{48,64},{64,80},{80,96},{96,112},{112,128},... | collective-permute-start | bytes 12296 | tf_op jit(solution)/shard_map/ppermute | solution.py:25
  305.1 6.3 collective-permute-start.4
  312.1 18.1 %all_gather.64 = f32[8,1024]{1,0:T(8,128)S(1)} all-gather(f32[8,128]{1,0:T(8,128)S(1)} %collective-permute-done.4), channel_id=1, replica_groups=mesh['tm'=16,'blk'=8,'samp'=2] {'blk'}, dimensions={1}, use_global_device_ids=true | all-gather | bytes 36864 | tf_op jit(solution)/shard_map/all_gather | solution.py:102
  332.7 2.4 collective-permute-done.6
  335.1 18.1 %all_gather.66 = f32[8,1024]{1,0:T(8,128)S(1)} all-gather(f32[8,128]{1,0:T(8,128)S(1)} %collective-permute-done.6), channel_id=1, replica_groups=mesh['tm'=16,'blk'=8,'samp'=2] {'blk'}, dimensions={1}, use_global_device_ids=true | all-gather | bytes 36864 | tf_op jit(solution)/shard_map/all_gather | solution.py:102
  353.6 2.2 collective-permute-start.8
  359.5 18.3 %all_gather.68 = f32[8,1024]{1,0:T(8,128)S(1)} all-gather(f32[8,128]{1,0:T(8,128)S(1)} %collective-permute-done.8), channel_id=1, replica_groups=mesh['tm'=16,'blk'=8,'samp'=2] {'blk'}, dimensions={1}, use_global_device_ids=true | all-gather | bytes 36864 | tf_op jit(solution)/shard_map/all_gather | solution.py:102
  381.8 18.1 %all_gather.70 = f32[8,1024]{1,0:T(8,128)S(1)} all-gather(f32[8,128]{1,0:T(8,128)S(1)} %collective-permute-done.10), channel_id=1, replica_groups=mesh['tm'=16,'blk'=8,'samp'=2] {'blk'}, dimensions={1}, use_global_device_ids=true | all-gather | bytes 36864 | tf_op jit(solution)/shard_map/all_gather | solution.py:102
  399.9 4.6 fusion.31
  405.0 18.2 %all_gather.72 = f32[8,1024]{1,0:T(8,128)S(1)} all-gather(f32[8,128]{1,0:T(8,128)S(1)} %convolution_add_fusion.7), channel_id=1, replica_groups=mesh['tm'=16,'blk'=8,'samp'=2] {'blk'}, dimensions={1}, use_global_device_ids=true | all-gather | bytes 36864 | tf_op jit(solution)/shard_map/all_gather | solution.py:108
  424.2 18.2 %all_gather.73 = f32[2,8,1024]{2,1,0:T(8,128)S(1)} all-gather(f32[2,8,128]{2,1,0:T(8,128)S(1)} %fusion.18), channel_id=1, replica_groups=mesh['tm'=16,'blk'=8,'samp'=2] {'blk'}, dimensions={2}, use_global_device_ids=true | all-gather | bytes 73728 | tf_op jit(solution)/shard_map/all_gather | solution.py:117
  442.9 18.1 %all_gather.74 = f32[8,1024]{1,0:T(8,128)S(1)} all-gather(f32[8,128]{1,0:T(8,128)S(1)} %fusion.19), channel_id=1, replica_groups=mesh['tm'=16,'blk'=8,'samp'=2] {'blk'}, dimensions={1}, use_global_device_ids=true | all-gather | bytes 36864 | tf_op jit(solution)/shard_map/all_gather | solution.py:121
  461.3 483.5 %while.14 = (s32[]{:T(128)}, f32[8,1024]{1,0:T(8,128)S(1)}, f32[128,1024]{1,0:T(8,128)S(1)}, f32[8,128]{1,0:T(8,128)S(1)}, s32[]{:T(128)}, /*index=5*/s32[]{:T(128)}, u32[]{:T(128)}, u32[]{:T(128)}, s32[]{:T(128)}) while((s32[]{:T(128)}, f32[8,1024]{1,0:T(8,128)S(1)}, f32[128,1024]{1,0:T(8,128)S(1)}, f32[8,128]{1,0:T(8,128)S(1)}, ...), condition=%wide.region_2.3_spmd.clone, body=%wide.region_1.2_spmd.clone.sunk | while | flops 12608520 | bytes 831686 | solution.py:130
  461.8 18.2 %all_gather.77 = f32[8,1024]{1,0:T(8,128)S(1)} all-gather(f32[8,128]{1,0:T(8,128)S(1)} %convolution_add_fusion.12), channel_id=1, replica_groups=mesh['tm'=16,'blk'=8,'samp'=2] {'blk'}, dimensions={1}, use_global_device_ids=true | all-gather | bytes 36864 | tf_op jit(solution)/shard_map/while/body/eval_jaxpr/all_gather | solution.py:126
  480.0 57.5 %collective-permute-start = (f32[8,1024]{1,0:T(8,128)S(1)}, f32[8,1024]{1,0:T(8,128)S(1)}, u32[]{:S(2)}, u32[]{:S(2)}) collective-permute-start(f32[8,1024]{1,0:T(8,128)S(1)} %all_gather.77), channel_id=1, source_target_pairs={{16,0},{32,16},{48,32},{64,48},{80,64},{96,80},{112,96},{128,112},... | collective-permute-start | bytes 98312 | tf_op jit(solution)/shard_map/while/body/eval_jaxpr/ppermute | solution.py:25
  537.5 8.6 collective-permute-done
  546.5 18.2 %all_gather.77 = f32[8,1024]{1,0:T(8,128)S(1)} all-gather(f32[8,128]{1,0:T(8,128)S(1)} %convolution_add_fusion.12), channel_id=1, replica_groups=mesh['tm'=16,'blk'=8,'samp'=2] {'blk'}, dimensions={1}, use_global_device_ids=true | all-gather | bytes 36864 | tf_op jit(solution)/shard_map/while/body/eval_jaxpr/all_gather | solution.py:126
  566.6 7.9 collective-permute-done
  575.0 18.2 %all_gather.77 = f32[8,1024]{1,0:T(8,128)S(1)} all-gather(f32[8,128]{1,0:T(8,128)S(1)} %convolution_add_fusion.12), channel_id=1, replica_groups=mesh['tm'=16,'blk'=8,'samp'=2] {'blk'}, dimensions={1}, use_global_device_ids=true | all-gather | bytes 36864 | tf_op jit(solution)/shard_map/while/body/eval_jaxpr/all_gather | solution.py:126
  595.1 7.9 collective-permute-done
  603.4 18.2 %all_gather.77 = f32[8,1024]{1,0:T(8,128)S(1)} all-gather(f32[8,128]{1,0:T(8,128)S(1)} %convolution_add_fusion.12), channel_id=1, replica_groups=mesh['tm'=16,'blk'=8,'samp'=2] {'blk'}, dimensions={1}, use_global_device_ids=true | all-gather | bytes 36864 | tf_op jit(solution)/shard_map/while/body/eval_jaxpr/all_gather | solution.py:126
  623.5 7.9 collective-permute-done
  631.9 18.2 %all_gather.77 = f32[8,1024]{1,0:T(8,128)S(1)} all-gather(f32[8,128]{1,0:T(8,128)S(1)} %convolution_add_fusion.12), channel_id=1, replica_groups=mesh['tm'=16,'blk'=8,'samp'=2] {'blk'}, dimensions={1}, use_global_device_ids=true | all-gather | bytes 36864 | tf_op jit(solution)/shard_map/while/body/eval_jaxpr/all_gather | solution.py:126
  652.0 7.9 collective-permute-done
  660.4 18.2 %all_gather.77 = f32[8,1024]{1,0:T(8,128)S(1)} all-gather(f32[8,128]{1,0:T(8,128)S(1)} %convolution_add_fusion.12), channel_id=1, replica_groups=mesh['tm'=16,'blk'=8,'samp'=2] {'blk'}, dimensions={1}, use_global_device_ids=true | all-gather | bytes 36864 | tf_op jit(solution)/shard_map/while/body/eval_jaxpr/all_gather | solution.py:126
  680.5 7.9 collective-permute-done
  688.9 18.2 %all_gather.77 = f32[8,1024]{1,0:T(8,128)S(1)} all-gather(f32[8,128]{1,0:T(8,128)S(1)} %convolution_add_fusion.12), channel_id=1, replica_groups=mesh['tm'=16,'blk'=8,'samp'=2] {'blk'}, dimensions={1}, use_global_device_ids=true | all-gather | bytes 36864 | tf_op jit(solution)/shard_map/while/body/eval_jaxpr/all_gather | solution.py:126
  709.0 7.9 collective-permute-done
  717.4 18.2 %all_gather.77 = f32[8,1024]{1,0:T(8,128)S(1)} all-gather(f32[8,128]{1,0:T(8,128)S(1)} %convolution_add_fusion.12), channel_id=1, replica_groups=mesh['tm'=16,'blk'=8,'samp'=2] {'blk'}, dimensions={1}, use_global_device_ids=true | all-gather | bytes 36864 | tf_op jit(solution)/shard_map/while/body/eval_jaxpr/all_gather | solution.py:126
  737.5 7.9 collective-permute-done
  745.9 18.2 %all_gather.77 = f32[8,1024]{1,0:T(8,128)S(1)} all-gather(f32[8,128]{1,0:T(8,128)S(1)} %convolution_add_fusion.12), channel_id=1, replica_groups=mesh['tm'=16,'blk'=8,'samp'=2] {'blk'}, dimensions={1}, use_global_device_ids=true | all-gather | bytes 36864 | tf_op jit(solution)/shard_map/while/body/eval_jaxpr/all_gather | solution.py:126
  766.0 7.9 collective-permute-done
  774.3 18.2 %all_gather.77 = f32[8,1024]{1,0:T(8,128)S(1)} all-gather(f32[8,128]{1,0:T(8,128)S(1)} %convolution_add_fusion.12), channel_id=1, replica_groups=mesh['tm'=16,'blk'=8,'samp'=2] {'blk'}, dimensions={1}, use_global_device_ids=true | all-gather | bytes 36864 | tf_op jit(solution)/shard_map/while/body/eval_jaxpr/all_gather | solution.py:126
  794.5 7.9 collective-permute-done
  802.8 18.2 %all_gather.77 = f32[8,1024]{1,0:T(8,128)S(1)} all-gather(f32[8,128]{1,0:T(8,128)S(1)} %convolution_add_fusion.12), channel_id=1, replica_groups=mesh['tm'=16,'blk'=8,'samp'=2] {'blk'}, dimensions={1}, use_global_device_ids=true | all-gather | bytes 36864 | tf_op jit(solution)/shard_map/while/body/eval_jaxpr/all_gather | solution.py:126
  822.9 7.9 collective-permute-done
  831.3 18.2 %all_gather.77 = f32[8,1024]{1,0:T(8,128)S(1)} all-gather(f32[8,128]{1,0:T(8,128)S(1)} %convolution_add_fusion.12), channel_id=1, replica_groups=mesh['tm'=16,'blk'=8,'samp'=2] {'blk'}, dimensions={1}, use_global_device_ids=true | all-gather | bytes 36864 | tf_op jit(solution)/shard_map/while/body/eval_jaxpr/all_gather | solution.py:126
  851.4 7.9 collective-permute-done
  859.8 18.2 %all_gather.77 = f32[8,1024]{1,0:T(8,128)S(1)} all-gather(f32[8,128]{1,0:T(8,128)S(1)} %convolution_add_fusion.12), channel_id=1, replica_groups=mesh['tm'=16,'blk'=8,'samp'=2] {'blk'}, dimensions={1}, use_global_device_ids=true | all-gather | bytes 36864 | tf_op jit(solution)/shard_map/while/body/eval_jaxpr/all_gather | solution.py:126
  879.9 7.9 collective-permute-done
  888.3 18.2 %all_gather.77 = f32[8,1024]{1,0:T(8,128)S(1)} all-gather(f32[8,128]{1,0:T(8,128)S(1)} %convolution_add_fusion.12), channel_id=1, replica_groups=mesh['tm'=16,'blk'=8,'samp'=2] {'blk'}, dimensions={1}, use_global_device_ids=true | all-gather | bytes 36864 | tf_op jit(solution)/shard_map/while/body/eval_jaxpr/all_gather | solution.py:126
  908.4 7.9 collective-permute-done
  916.8 18.2 %all_gather.77 = f32[8,1024]{1,0:T(8,128)S(1)} all-gather(f32[8,128]{1,0:T(8,128)S(1)} %convolution_add_fusion.12), channel_id=1, replica_groups=mesh['tm'=16,'blk'=8,'samp'=2] {'blk'}, dimensions={1}, use_global_device_ids=true | all-gather | bytes 36864 | tf_op jit(solution)/shard_map/while/body/eval_jaxpr/all_gather | solution.py:126
  936.9 7.9 collective-permute-done
  (139 shorter events, 55.5 us)
Async XLA Ops:
  6.5 51.7 %all-gather.17.cloned.1.call-start = ((), (), s32[]{:S(2)}) async-start(), calls=%async_computation.4 | async-start | bytes 2359296 | tf_op jit(solution)/shard_map/all_gather | solution.py:80
  16.1 271.2 %copy-start = (bf16[2,128,1024]{2,1,0:T(8,128)(2,1)}, bf16[2,128,1024]{2,1,0:T(8,128)(2,1)S(1)}, u32[]{:S(2)}) copy-start(bf16[2,128,1024]{2,1,0:T(8,128)(2,1)S(1)} %all_gather.63) | copy-start | bytes 1572868
  16.9 144.4 %copy-start.7 = (bf16[2,128,512]{2,1,0:T(8,128)(2,1)S(1)}, bf16[2,128,512]{2,1,0:T(8,128)(2,1)}, u32[]{:S(2)}) copy-start(bf16[2,128,512]{2,1,0:T(8,128)(2,1)} %param.22) | copy-start | bytes 786436
  16.9 123.9 %all-gather.9.cloned.1.call-start = ((), (), s32[]{:S(2)}) async-start(), calls=%async_computation | async-start | bytes 4718592 | tf_op jit(solution)/shard_map/all_gather | solution.py:101
  60.2 13.5 %copy-start.2 = (f32[128,1024]{1,0:T(8,128)}, f32[128,1024]{1,0:T(8,128)S(1)}, u32[]{:S(2)}) copy-start(f32[128,1024]{1,0:T(8,128)S(1)} %fusion.4) | copy-start | bytes 1572868
  60.3 13.5 %collective-permute-start.5 = (f32[128,1024]{1,0:T(8,128)S(1)}, f32[128,1024]{1,0:T(8,128)S(1)}, u32[]{:S(2)}, u32[]{:S(2)}) collective-permute-start(f32[128,1024]{1,0:T(8,128)S(1)} %fusion.4), channel_id=1, source_target_pairs={{0,16},{16,32},{32,48},{48,64},{64,80},{80,96},{96,112},{112,128},... | collective-permute-start | bytes 1572872 | tf_op jit(solution)/shard_map/ppermute | solution.py:25
  73.7 12.6 %collective-permute-start.7 = (f32[128,1024]{1,0:T(8,128)S(1)}, f32[128,1024]{1,0:T(8,128)S(1)}, u32[]{:S(2)}, u32[]{:S(2)}) collective-permute-start(f32[128,1024]{1,0:T(8,128)S(1)} %collective-permute-done.5), channel_id=1, source_target_pairs={{0,16},{16,32},{32,48},{48,64},{64,80},{80,96},{96,112},{112,128},... | collective-permute-start | bytes 1572872 | tf_op jit(solution)/shard_map/ppermute | solution.py:25
  86.3 0.8 copy-start.6
  87.2 128.5 %all-gather.11.cloned.1.call-start = ((), (), s32[]{:S(2)}) async-start(), calls=%async_computation.1 | async-start | bytes 4718592 | tf_op jit(solution)/shard_map/all_gather | solution.py:101
  145.4 91.9 %copy-start.8 = (f32[2,8,32]{2,1,0:T(8,128)S(1)}, f32[2,8,32]{2,1,0:T(8,128)}, u32[]{:S(2)}) copy-start(f32[2,8,32]{2,1,0:T(8,128)} %param.16) | copy-start | bytes 6148
  145.4 94.6 %copy-start.16 = (s32[16]{0:T(128)S(1)}, s32[16]{0:T(128)}, u32[]{:S(2)}) copy-start(s32[16]{0:T(128)} %param.18) | copy-start | bytes 196
  145.4 94.6 %copy-start.9 = (bf16[2,128,128]{2,1,0:T(8,128)(2,1)S(1)}, bf16[2,128,128]{2,1,0:T(8,128)(2,1)}, u32[]{:S(2)}) copy-start(bf16[2,128,128]{2,1,0:T(8,128)(2,1)} %param.21) | copy-start | bytes 196612
  145.5 100.0 %copy-start.10 = (f32[16,8,8]{0,2,1:T(8,128)S(1)}, f32[16,8,8]{0,2,1:T(8,128)}, u32[]{:S(2)}) copy-start(f32[16,8,8]{0,2,1:T(8,128)} %param.17) | copy-start | bytes 12292
  145.5 100.1 %copy-start.11 = (f32[2,8,128]{2,1,0:T(8,128)S(1)}, f32[2,8,128]{2,1,0:T(8,128)}, u32[]{:S(2)}) copy-start(f32[2,8,128]{2,1,0:T(8,128)} %param.13) | copy-start | bytes 24580
  145.5 14.8 %collective-permute-start.9 = (f32[128,1024]{1,0:T(8,128)S(1)}, f32[128,1024]{1,0:T(8,128)S(1)}, u32[]{:S(2)}, u32[]{:S(2)}) collective-permute-start(f32[128,1024]{1,0:T(8,128)S(1)} %fusion.29), channel_id=1, source_target_pairs={{0,32},{16,48},{32,64},{48,80},{64,96},{80,112},{96,128},{112,144}... | collective-permute-start | bytes 1572872 | tf_op jit(solution)/shard_map/ppermute | solution.py:25
  160.3 0.8 copy-start.5
  160.3 85.4 %copy-start.15 = (s32[2,4]{1,0:T(2,128)S(1)}, s32[2,4]{1,0:T(2,128)}, u32[]{:S(2)}) copy-start(s32[2,4]{1,0:T(2,128)} %param.15) | copy-start | bytes 100
  161.2 85.6 %copy-start.14 = (f32[2,32]{1,0:T(2,128)S(1)}, f32[2,32]{1,0:T(2,128)}, u32[]{:S(2)}) copy-start(f32[2,32]{1,0:T(2,128)} %param.14) | copy-start | bytes 772
  161.2 218.6 %all-gather.15.cloned.1.call-start = ((), (), s32[]{:S(2)}) async-start(), calls=%async_computation.3 | async-start | bytes 2359296 | tf_op jit(solution)/shard_map/all_gather | solution.py:85
  170.4 134.7 %copy-start.12 = (f32[8,128]{1,0:T(8,128)S(1)}, f32[8,128]{1,0:T(8,128)}, u32[]{:S(2)}) copy-start(f32[8,128]{1,0:T(8,128)} %param.19) | copy-start | bytes 12292
  170.5 185.3 %copy-start.13 = (f32[4,4]{1,0:T(4,128)S(1)}, f32[4,4]{1,0:T(4,128)}, u32[]{:S(2)}) copy-start(f32[4,4]{1,0:T(4,128)} %param.23) | copy-start | bytes 196
  170.5 229.5 %all-gather.13.cloned.1.call-start = ((), (), s32[]{:S(2)}) async-start(), calls=%async_computation.2 | async-start | bytes 4718592 | tf_op jit(solution)/shard_map/all_gather | solution.py:101
  220.2 16.2 %collective-permute-start.11 = (f32[128,1024]{1,0:T(8,128)S(1)}, f32[128,1024]{1,0:T(8,128)S(1)}, u32[]{:S(2)}, u32[]{:S(2)}) collective-permute-start(f32[128,1024]{1,0:T(8,128)S(1)} %fusion.30), channel_id=1, source_target_pairs={{0,64},{16,80},{32,96},{48,112},{64,128},{80,144},{96,160},{112,17... | collective-permute-start | bytes 1572872 | tf_op jit(solution)/shard_map/ppermute | solution.py:25
  236.4 0.8 copy-start.4
  237.4 8.5 collective-permute-start.1
  237.4 8.5 collective-permute-start.2
  287.5 17.6 %collective-permute-start.3 = (f32[8,128]{1,0:T(8,128)S(1)}, f32[8,128]{1,0:T(8,128)S(1)}, u32[]{:S(2)}, u32[]{:S(2)}) collective-permute-start(f32[8,128]{1,0:T(8,128)S(1)} %convolution_add_fusion.4), channel_id=1, source_target_pairs={{0,16},{16,32},{32,48},{48,64},{64,80},{80,96},{96,112},{112,128},... | collective-permute-start | bytes 12296 | tf_op jit(solution)/shard_map/ppermute | solution.py:25
  305.1 7.0 collective-permute-start.4
  330.6 4.4 collective-permute-start.6
  353.6 5.9 collective-permute-start.8
  378.2 44.9 %copy-start.1 = (bf16[2,128,1024]{2,1,0:T(8,128)(2,1)S(1)}, bf16[2,128,1024]{2,1,0:T(8,128)(2,1)}, u32[]{:S(2)}) copy-start(bf16[2,128,1024]{2,1,0:T(8,128)(2,1)} %copy-done) | copy-start | bytes 1572868
  378.3 45.1 %copy-start.3 = (f32[128,1024]{1,0:T(8,128)S(1)}, f32[128,1024]{1,0:T(8,128)}, u32[]{:S(2)}) copy-start(f32[128,1024]{1,0:T(8,128)} %copy-done.2) | copy-start | bytes 1572868
  378.3 3.5 collective-permute-start.10
  480.0 66.1 %collective-permute-start = (f32[8,1024]{1,0:T(8,128)S(1)}, f32[8,1024]{1,0:T(8,128)S(1)}, u32[]{:S(2)}, u32[]{:S(2)}) collective-permute-start(f32[8,1024]{1,0:T(8,128)S(1)} %all_gather.77), channel_id=1, source_target_pairs={{16,0},{32,16},{48,32},{64,48},{80,64},{96,80},{112,96},{128,112},... | collective-permute-start | bytes 98312 | tf_op jit(solution)/shard_map/while/body/eval_jaxpr/ppermute | solution.py:25
  564.7 9.9 %collective-permute-start = (f32[8,1024]{1,0:T(8,128)S(1)}, f32[8,1024]{1,0:T(8,128)S(1)}, u32[]{:S(2)}, u32[]{:S(2)}) collective-permute-start(f32[8,1024]{1,0:T(8,128)S(1)} %all_gather.77), channel_id=1, source_target_pairs={{16,0},{32,16},{48,32},{64,48},{80,64},{96,80},{112,96},{128,112},... | collective-permute-start | bytes 98312 | tf_op jit(solution)/shard_map/while/body/eval_jaxpr/ppermute | solution.py:25
  593.1 9.9 %collective-permute-start = (f32[8,1024]{1,0:T(8,128)S(1)}, f32[8,1024]{1,0:T(8,128)S(1)}, u32[]{:S(2)}, u32[]{:S(2)}) collective-permute-start(f32[8,1024]{1,0:T(8,128)S(1)} %all_gather.77), channel_id=1, source_target_pairs={{16,0},{32,16},{48,32},{64,48},{80,64},{96,80},{112,96},{128,112},... | collective-permute-start | bytes 98312 | tf_op jit(solution)/shard_map/while/body/eval_jaxpr/ppermute | solution.py:25
  621.6 9.9 %collective-permute-start = (f32[8,1024]{1,0:T(8,128)S(1)}, f32[8,1024]{1,0:T(8,128)S(1)}, u32[]{:S(2)}, u32[]{:S(2)}) collective-permute-start(f32[8,1024]{1,0:T(8,128)S(1)} %all_gather.77), channel_id=1, source_target_pairs={{16,0},{32,16},{48,32},{64,48},{80,64},{96,80},{112,96},{128,112},... | collective-permute-start | bytes 98312 | tf_op jit(solution)/shard_map/while/body/eval_jaxpr/ppermute | solution.py:25
  650.1 9.9 %collective-permute-start = (f32[8,1024]{1,0:T(8,128)S(1)}, f32[8,1024]{1,0:T(8,128)S(1)}, u32[]{:S(2)}, u32[]{:S(2)}) collective-permute-start(f32[8,1024]{1,0:T(8,128)S(1)} %all_gather.77), channel_id=1, source_target_pairs={{16,0},{32,16},{48,32},{64,48},{80,64},{96,80},{112,96},{128,112},... | collective-permute-start | bytes 98312 | tf_op jit(solution)/shard_map/while/body/eval_jaxpr/ppermute | solution.py:25
  678.6 9.9 %collective-permute-start = (f32[8,1024]{1,0:T(8,128)S(1)}, f32[8,1024]{1,0:T(8,128)S(1)}, u32[]{:S(2)}, u32[]{:S(2)}) collective-permute-start(f32[8,1024]{1,0:T(8,128)S(1)} %all_gather.77), channel_id=1, source_target_pairs={{16,0},{32,16},{48,32},{64,48},{80,64},{96,80},{112,96},{128,112},... | collective-permute-start | bytes 98312 | tf_op jit(solution)/shard_map/while/body/eval_jaxpr/ppermute | solution.py:25
  707.1 9.9 %collective-permute-start = (f32[8,1024]{1,0:T(8,128)S(1)}, f32[8,1024]{1,0:T(8,128)S(1)}, u32[]{:S(2)}, u32[]{:S(2)}) collective-permute-start(f32[8,1024]{1,0:T(8,128)S(1)} %all_gather.77), channel_id=1, source_target_pairs={{16,0},{32,16},{48,32},{64,48},{80,64},{96,80},{112,96},{128,112},... | collective-permute-start | bytes 98312 | tf_op jit(solution)/shard_map/while/body/eval_jaxpr/ppermute | solution.py:25
  735.6 9.9 %collective-permute-start = (f32[8,1024]{1,0:T(8,128)S(1)}, f32[8,1024]{1,0:T(8,128)S(1)}, u32[]{:S(2)}, u32[]{:S(2)}) collective-permute-start(f32[8,1024]{1,0:T(8,128)S(1)} %all_gather.77), channel_id=1, source_target_pairs={{16,0},{32,16},{48,32},{64,48},{80,64},{96,80},{112,96},{128,112},... | collective-permute-start | bytes 98312 | tf_op jit(solution)/shard_map/while/body/eval_jaxpr/ppermute | solution.py:25
  764.0 9.9 %collective-permute-start = (f32[8,1024]{1,0:T(8,128)S(1)}, f32[8,1024]{1,0:T(8,128)S(1)}, u32[]{:S(2)}, u32[]{:S(2)}) collective-permute-start(f32[8,1024]{1,0:T(8,128)S(1)} %all_gather.77), channel_id=1, source_target_pairs={{16,0},{32,16},{48,32},{64,48},{80,64},{96,80},{112,96},{128,112},... | collective-permute-start | bytes 98312 | tf_op jit(solution)/shard_map/while/body/eval_jaxpr/ppermute | solution.py:25
  792.5 9.9 %collective-permute-start = (f32[8,1024]{1,0:T(8,128)S(1)}, f32[8,1024]{1,0:T(8,128)S(1)}, u32[]{:S(2)}, u32[]{:S(2)}) collective-permute-start(f32[8,1024]{1,0:T(8,128)S(1)} %all_gather.77), channel_id=1, source_target_pairs={{16,0},{32,16},{48,32},{64,48},{80,64},{96,80},{112,96},{128,112},... | collective-permute-start | bytes 98312 | tf_op jit(solution)/shard_map/while/body/eval_jaxpr/ppermute | solution.py:25
  821.0 9.9 %collective-permute-start = (f32[8,1024]{1,0:T(8,128)S(1)}, f32[8,1024]{1,0:T(8,128)S(1)}, u32[]{:S(2)}, u32[]{:S(2)}) collective-permute-start(f32[8,1024]{1,0:T(8,128)S(1)} %all_gather.77), channel_id=1, source_target_pairs={{16,0},{32,16},{48,32},{64,48},{80,64},{96,80},{112,96},{128,112},... | collective-permute-start | bytes 98312 | tf_op jit(solution)/shard_map/while/body/eval_jaxpr/ppermute | solution.py:25
  849.5 9.9 %collective-permute-start = (f32[8,1024]{1,0:T(8,128)S(1)}, f32[8,1024]{1,0:T(8,128)S(1)}, u32[]{:S(2)}, u32[]{:S(2)}) collective-permute-start(f32[8,1024]{1,0:T(8,128)S(1)} %all_gather.77), channel_id=1, source_target_pairs={{16,0},{32,16},{48,32},{64,48},{80,64},{96,80},{112,96},{128,112},... | collective-permute-start | bytes 98312 | tf_op jit(solution)/shard_map/while/body/eval_jaxpr/ppermute | solution.py:25
  878.0 9.9 %collective-permute-start = (f32[8,1024]{1,0:T(8,128)S(1)}, f32[8,1024]{1,0:T(8,128)S(1)}, u32[]{:S(2)}, u32[]{:S(2)}) collective-permute-start(f32[8,1024]{1,0:T(8,128)S(1)} %all_gather.77), channel_id=1, source_target_pairs={{16,0},{32,16},{48,32},{64,48},{80,64},{96,80},{112,96},{128,112},... | collective-permute-start | bytes 98312 | tf_op jit(solution)/shard_map/while/body/eval_jaxpr/ppermute | solution.py:25
  906.5 9.9 %collective-permute-start = (f32[8,1024]{1,0:T(8,128)S(1)}, f32[8,1024]{1,0:T(8,128)S(1)}, u32[]{:S(2)}, u32[]{:S(2)}) collective-permute-start(f32[8,1024]{1,0:T(8,128)S(1)} %all_gather.77), channel_id=1, source_target_pairs={{16,0},{32,16},{48,32},{64,48},{80,64},{96,80},{112,96},{128,112},... | collective-permute-start | bytes 98312 | tf_op jit(solution)/shard_map/while/body/eval_jaxpr/ppermute | solution.py:25
  934.9 9.9 %collective-permute-start = (f32[8,1024]{1,0:T(8,128)S(1)}, f32[8,1024]{1,0:T(8,128)S(1)}, u32[]{:S(2)}, u32[]{:S(2)}) collective-permute-start(f32[8,1024]{1,0:T(8,128)S(1)} %all_gather.77), channel_id=1, source_target_pairs={{16,0},{32,16},{48,32},{64,48},{80,64},{96,80},{112,96},{128,112},... | collective-permute-start | bytes 98312 | tf_op jit(solution)/shard_map/while/body/eval_jaxpr/ppermute | solution.py:25
Sparse Core Ops, SparseCore 0:
  17.0 41.1 all-gather.16
  87.3 53.4 all-gather.8
  161.3 54.2 all-gather.10
  217.3 36.5 all-gather.14
  255.5 56.7 all-gather.12
where the time goes:
time: 954 us; the launch traced here: 953 us
  blocking collectives  463 us (49%)
  waiting for transfers between devices  301 us (32%)
  starting transfers between devices  137 us (14%)
  matrix products  29.7 us (3%)
  between operations  13.6 us (1%)
    all_gather x15, blocking collectives, relay_back(): complete = lax.all_gather(emitted, 'blk', axis=1, tiled=True)  273 us
    ppermute x24, waiting for transfers between devices, shifted(): lax.ppermute(value, axis, [(source, source + steps) for source in range(i...  161 us
    ppermute x24, starting transfers between devices, shifted(): lax.ppermute(value, axis, [(source, source + steps) for source in range(i...  134 us
    all_gather x3, waiting for transfers between devices, on_device(): lax.all_gather(received_m, 'blk', axis=0, tiled=True)  98.7 us
    all_gather x4, blocking collectives, on_device(): lax.all_gather(received_v, 'blk', axis=1, tiled=True)  72.5 us
    all_gather x1, waiting for transfers between devices, on_device(): lax.all_gather(trans_mats[0], 'blk', axis=0, tiled=True)  41.3 us
    all_gather x1, blocking collectives, on_device(): lax.all_gather(inputs[0], 'blk', axis=1, tiled=True)  20.3 us
    all_gather x1, blocking collectives, on_device(): all_resid = lax.all_gather(residual, 'blk', axis=2, tiled=True)  19.8 us
  transfers between devices with their start and end apart: 31, of which 26 were waited for; matrix products, arithmetic and copies ran while one was open for 1% of the time, Pallas kernels for 0%

commit v1 on v0

--- a/solution.py
+++ b/solution.py
@@ -123,7 +123,11 @@
 
     def relay_back(relay_turn, later_now):
         emitted = apply_rows(backward_pair, later_now) + back_offset
-        complete = lax.all_gather(emitted, "blk", axis=1, tiled=True)
+        peers = lax.axis_size("blk")
+        repeats = [peers if d == 1 else 1 for d in range(emitted.ndim)]
+        complete = lax.all_to_all(
+            jnp.tile(emitted, repeats), "blk", split_axis=1, concat_axis=1, tiled=True
+        )
         received = shifted(complete, "tm", -1)
         return jnp.where(lax.axis_index("tm") == time_size - 2 - relay_turn, received, later_now)
 

time: 954 us -> 783 us (0.82)
  blocking collectives: 463 us -> 330 us
  waiting for transfers between devices: 301 us -> 266 us
    all_gather x15 -> x0, blocking collectives: 273 us -> none  [relay_back(): complete = lax.all_gather(emitted, 'blk', axis=1, tiled=True)]
    all_to_all x0 -> x15, blocking collectives: none -> 140 us  [relay_back(): lax.all_to_all(jnp.tile(emitted, repeats), 'blk', split_axis=1, concat_ax...]
    ppermute x24, waiting for transfers between devices: 161 us -> 126 us  [shifted(): lax.ppermute(value, axis, [(source, source + steps) for source in range(i...]
  transfers between devices with their start and end apart: 31 -> 31, of which waited for: 26 -> 26; matrix products, arithmetic and copies ran while one was open for 1% -> 2% of each run, Pallas kernels for 0% -> 0%
where the time goes in v1:
time: 783 us; the launch traced here: 781 us
  blocking collectives  330 us (42%)
  waiting for transfers between devices  266 us (34%)
  starting transfers between devices  132 us (17%)
  matrix products  29.7 us (4%)
  between operations  13.6 us (2%)
  local copies, waits for them, and re-layouts  7.9 us (1%)
    all_to_all x15, blocking collectives, relay_back(): lax.all_to_all(jnp.tile(emitted, repeats), 'blk', split_axis=1, concat_ax...  140 us
    ppermute x24, starting transfers between devices, shifted(): lax.ppermute(value, axis, [(source, source + steps) for source in range(i...  129 us
    ppermute x24, waiting for transfers between devices, shifted(): lax.ppermute(value, axis, [(source, source + steps) for source in range(i...  126 us
    all_gather x3, waiting for transfers between devices, on_device(): lax.all_gather(received_m, 'blk', axis=0, tiled=True)  98.7 us
    all_gather x4, blocking collectives, on_device(): lax.all_gather(received_v, 'blk', axis=1, tiled=True)  72.5 us
    all_gather x1, waiting for transfers between devices, on_device(): lax.all_gather(trans_mats[0], 'blk', axis=0, tiled=True)  41.3 us
    all_gather x1, blocking collectives, on_device(): lax.all_gather(inputs[0], 'blk', axis=1, tiled=True)  20.3 us
    all_gather x1, blocking collectives, on_device(): all_resid = lax.all_gather(residual, 'blk', axis=2, tiled=True)  19.8 us
  transfers between devices with their start and end apart: 31, of which 26 were waited for; matrix products, arithmetic and copies ran while one was open for 2% of the time, Pallas kernels for 0%

profile of v1, /device:TPU:7, one launch (start us, length us, event | category | flops | bytes accessed | tf_op | source)
XLA Modules:
  0.0 781.4 jit_solution(9297745965805951463)
XLA Ops:
  6.5 9.6 %all_gather.56 = bf16[2,128,1024]{2,1,0:T(8,128)(2,1)S(1)} all-gather(bf16[2,128,512]{2,1,0:T(8,128)(2,1)} %param.20), channel_id=1, replica_groups=mesh['tm'=16,'blk'=8,'samp'=2] {'samp'}, dimensions={2}, use_global_device_ids=true | all-gather | bytes 786432 | tf_op jit(solution)/shard_map/all_gather | solution.py:46
  16.9 41.3 %all-gather.17.cloned.1.call-done = bf16[1,1024,1024]{2,1,0:T(8,128)(2,1)} async-done(((bf16[1,128,1024]{2,1,0:T(8,128)(2,1)}), bf16[1,1024,1024]{2,1,0:T(8,128)(2,1)}) %all-gather.17.cloned.1.call-update) | async-done | bytes 2097168 | tf_op jit(solution)/shard_map/all_gather | solution.py:80
  58.2 2.0 fusion.4
  60.3 7.4 collective-permute-start.5
  67.6 6.1 collective-permute-done.5
  73.7 6.5 collective-permute-start.7
  80.2 6.1 collective-permute-done.7
  87.2 53.6 %all-gather.9.cloned.1.call-done = f32[1024,1024]{1,0:T(8,128)} async-done(((f32[128,1024]{1,0:T(8,128)}), f32[1024,1024]{1,0:T(8,128)}) %all-gather.9.cloned.1.call-update) | async-done | bytes 4194320 | tf_op jit(solution)/shard_map/all_gather | solution.py:101
  140.8 4.6 fusion.29
  145.5 3.2 collective-permute-start.9
  148.7 11.6 %collective-permute-done.9 = f32[128,1024]{1,0:T(8,128)S(1)} collective-permute-done((f32[128,1024]{1,0:T(8,128)S(1)}, f32[128,1024]{1,0:T(8,128)S(1)}, u32[]{:S(2)}, u32[]{:S(2)}) %collective-permute-start.9) | collective-permute-done | bytes 524320 | tf_op jit(solution)/shard_map/ppermute | solution.py:25
  161.2 8.4 %all_gather.51 = bf16[2,128,1024]{2,1,0:T(8,128)(2,1)S(1)} all-gather(bf16[2,128,512]{2,1,0:T(8,128)(2,1)S(1)} %copy-done.7), channel_id=1, replica_groups=mesh['tm'=16,'blk'=8,'samp'=2] {'samp'}, dimensions={2}, use_global_device_ids=true | all-gather | bytes 786432 | tf_op jit(solution)/shard_map/all_gather | solution.py:48
  170.5 45.1 %all-gather.11.cloned.1.call-done = f32[1024,1024]{1,0:T(8,128)} async-done(((f32[128,1024]{1,0:T(8,128)}), f32[1024,1024]{1,0:T(8,128)}) %all-gather.11.cloned.1.call-update) | async-done | bytes 4194320 | tf_op jit(solution)/shard_map/all_gather | solution.py:101
  215.6 4.6 fusion.30
  220.2 4.0 collective-permute-start.11
  224.2 12.2 %collective-permute-done.11 = f32[128,1024]{1,0:T(8,128)S(1)} collective-permute-done((f32[128,1024]{1,0:T(8,128)S(1)}, f32[128,1024]{1,0:T(8,128)S(1)}, u32[]{:S(2)}, u32[]{:S(2)}) %collective-permute-start.11) | collective-permute-done | bytes 524320 | tf_op jit(solution)/shard_map/ppermute | solution.py:25
  237.4 2.7 collective-permute-start.2
  240.1 5.4 all_gather.54
  246.9 19.8 %all_gather.53 = f32[2,8,256]{1,0,2:T(2,128)S(1)} all-gather(f32[2,8,32]{1,0,2:T(2,128)S(1)} %copy.27), channel_id=1, replica_groups=mesh['tm'=16,'blk'=8,'samp'=2] {'blk'}, dimensions={2}, use_global_device_ids=true | all-gather | bytes 18432 | tf_op jit(solution)/shard_map/all_gather | solution.py:74
  267.0 20.3 %all-gather.1 = f32[1,8,1024]{2,1,0:T(8,128)S(1)} all-gather(f32[1,8,128]{2,1,0:T(8,128)S(1)} %slice.52), channel_id=3, replica_groups=mesh['tm'=16,'blk'=8,'samp'=2] {'blk'}, dimensions={2}, use_global_device_ids=true | all-gather | bytes 36864 | tf_op jit(solution)/shard_map/all_gather | solution.py:89
  287.5 16.8 %collective-permute-start.3 = (f32[8,128]{1,0:T(8,128)S(1)}, f32[8,128]{1,0:T(8,128)S(1)}, u32[]{:S(2)}, u32[]{:S(2)}) collective-permute-start(f32[8,128]{1,0:T(8,128)S(1)} %convolution_add_fusion.4), channel_id=1, source_target_pairs={{0,16},{16,32},{32,48},{48,64},{64,80},{80,96},{96,112},{112,128},... | collective-permute-start | bytes 12296 | tf_op jit(solution)/shard_map/ppermute | solution.py:25
  305.1 6.3 collective-permute-start.4
  312.1 18.1 %all_gather.57 = f32[8,1024]{1,0:T(8,128)S(1)} all-gather(f32[8,128]{1,0:T(8,128)S(1)} %collective-permute-done.4), channel_id=1, replica_groups=mesh['tm'=16,'blk'=8,'samp'=2] {'blk'}, dimensions={1}, use_global_device_ids=true | all-gather | bytes 36864 | tf_op jit(solution)/shard_map/all_gather | solution.py:102
  332.7 2.4 collective-permute-done.6
  335.1 18.1 %all_gather.59 = f32[8,1024]{1,0:T(8,128)S(1)} all-gather(f32[8,128]{1,0:T(8,128)S(1)} %collective-permute-done.6), channel_id=1, replica_groups=mesh['tm'=16,'blk'=8,'samp'=2] {'blk'}, dimensions={1}, use_global_device_ids=true | all-gather | bytes 36864 | tf_op jit(solution)/shard_map/all_gather | solution.py:102
  353.6 2.2 collective-permute-start.8
  359.5 18.3 %all_gather.61 = f32[8,1024]{1,0:T(8,128)S(1)} all-gather(f32[8,128]{1,0:T(8,128)S(1)} %collective-permute-done.8), channel_id=1, replica_groups=mesh['tm'=16,'blk'=8,'samp'=2] {'blk'}, dimensions={1}, use_global_device_ids=true | all-gather | bytes 36864 | tf_op jit(solution)/shard_map/all_gather | solution.py:102
  381.8 18.1 %all_gather.63 = f32[8,1024]{1,0:T(8,128)S(1)} all-gather(f32[8,128]{1,0:T(8,128)S(1)} %collective-permute-done.10), channel_id=1, replica_groups=mesh['tm'=16,'blk'=8,'samp'=2] {'blk'}, dimensions={1}, use_global_device_ids=true | all-gather | bytes 36864 | tf_op jit(solution)/shard_map/all_gather | solution.py:102
  399.9 4.6 fusion.31
  405.0 18.2 %all_gather.65 = f32[8,1024]{1,0:T(8,128)S(1)} all-gather(f32[8,128]{1,0:T(8,128)S(1)} %convolution_add_fusion.7), channel_id=1, replica_groups=mesh['tm'=16,'blk'=8,'samp'=2] {'blk'}, dimensions={1}, use_global_device_ids=true | all-gather | bytes 36864 | tf_op jit(solution)/shard_map/all_gather | solution.py:108
  424.2 18.2 %all_gather.66 = f32[2,8,1024]{2,1,0:T(8,128)S(1)} all-gather(f32[2,8,128]{2,1,0:T(8,128)S(1)} %fusion.18), channel_id=1, replica_groups=mesh['tm'=16,'blk'=8,'samp'=2] {'blk'}, dimensions={2}, use_global_device_ids=true | all-gather | bytes 73728 | tf_op jit(solution)/shard_map/all_gather | solution.py:117
  442.9 18.1 %all_gather.67 = f32[8,1024]{1,0:T(8,128)S(1)} all-gather(f32[8,128]{1,0:T(8,128)S(1)} %fusion.19), channel_id=1, replica_groups=mesh['tm'=16,'blk'=8,'samp'=2] {'blk'}, dimensions={1}, use_global_device_ids=true | all-gather | bytes 36864 | tf_op jit(solution)/shard_map/all_gather | solution.py:121
  461.3 312.2 %while.14 = (s32[]{:T(128)}, f32[8,1024]{1,0:T(8,128)S(1)}, f32[128,1024]{1,0:T(8,128)S(1)}, f32[8,128]{1,0:T(8,128)S(1)}, s32[]{:T(128)}, /*index=5*/s32[]{:T(128)}, u32[]{:T(128)}, u32[]{:T(128)}, s32[]{:T(128)}) while((s32[]{:T(128)}, f32[8,1024]{1,0:T(8,128)S(1)}, f32[128,1024]{1,0:T(8,128)S(1)}, f32[8,128]{1,0:T(8,128)S(1)}, ...), condition=%wide.region_2.3_spmd.clone, body=%wide.region_1.2_spmd.clone.sunk | while | flops 12608520 | bytes 897222 | solution.py:134
  461.9 10.5 %all_to_all.15 = f32[8,8,128]{2,0,1:T(8,128)S(1)} all-to-all(f32[8,8,128]{2,0,1:T(8,128)S(1)} %tile.19), channel_id=1, replica_groups=mesh['tm'=16,'blk'=8,'samp'=2] {'blk'}, dimensions={1} | all-to-all | bytes 65536 | tf_op jit(solution)/shard_map/while/body/eval_jaxpr/all_to_all | solution.py:128
  472.4 52.7 %collective-permute-start = (f32[8,1024]{1,0:T(8,128)S(1)}, f32[8,1024]{1,0:T(8,128)S(1)}, u32[]{:S(2)}, u32[]{:S(2)}) collective-permute-start(f32[8,1024]{1,0:T(8,128)S(1)} %bitcast.98), channel_id=1, source_target_pairs={{16,0},{32,16},{48,32},{64,48},{80,64},{96,80},{112,96},{128,112},... | collective-permute-start | bytes 98312 | tf_op jit(solution)/shard_map/while/body/eval_jaxpr/ppermute | solution.py:25
  525.1 8.7 %collective-permute-done = f32[8,1024]{1,0:T(8,128)S(1)} collective-permute-done((f32[8,1024]{1,0:T(8,128)S(1)}, f32[8,1024]{1,0:T(8,128)S(1)}, u32[]{:S(2)}, u32[]{:S(2)}) %collective-permute-start) | collective-permute-done | bytes 32800 | tf_op jit(solution)/shard_map/while/body/eval_jaxpr/ppermute | solution.py:25
  534.3 9.2 %all_to_all.15 = f32[8,8,128]{2,0,1:T(8,128)S(1)} all-to-all(f32[8,8,128]{2,0,1:T(8,128)S(1)} %tile.19), channel_id=1, replica_groups=mesh['tm'=16,'blk'=8,'samp'=2] {'blk'}, dimensions={1} | all-to-all | bytes 65536 | tf_op jit(solution)/shard_map/while/body/eval_jaxpr/all_to_all | solution.py:128
  545.5 5.4 collective-permute-done
  551.4 9.2 %all_to_all.15 = f32[8,8,128]{2,0,1:T(8,128)S(1)} all-to-all(f32[8,8,128]{2,0,1:T(8,128)S(1)} %tile.19), channel_id=1, replica_groups=mesh['tm'=16,'blk'=8,'samp'=2] {'blk'}, dimensions={1} | all-to-all | bytes 65536 | tf_op jit(solution)/shard_map/while/body/eval_jaxpr/all_to_all | solution.py:128
  562.6 5.4 collective-permute-done
  568.6 9.2 %all_to_all.15 = f32[8,8,128]{2,0,1:T(8,128)S(1)} all-to-all(f32[8,8,128]{2,0,1:T(8,128)S(1)} %tile.19), channel_id=1, replica_groups=mesh['tm'=16,'blk'=8,'samp'=2] {'blk'}, dimensions={1} | all-to-all | bytes 65536 | tf_op jit(solution)/shard_map/while/body/eval_jaxpr/all_to_all | solution.py:128
  579.7 5.4 collective-permute-done
  585.7 9.2 %all_to_all.15 = f32[8,8,128]{2,0,1:T(8,128)S(1)} all-to-all(f32[8,8,128]{2,0,1:T(8,128)S(1)} %tile.19), channel_id=1, replica_groups=mesh['tm'=16,'blk'=8,'samp'=2] {'blk'}, dimensions={1} | all-to-all | bytes 65536 | tf_op jit(solution)/shard_map/while/body/eval_jaxpr/all_to_all | solution.py:128
  596.8 5.4 collective-permute-done
  602.8 9.2 %all_to_all.15 = f32[8,8,128]{2,0,1:T(8,128)S(1)} all-to-all(f32[8,8,128]{2,0,1:T(8,128)S(1)} %tile.19), channel_id=1, replica_groups=mesh['tm'=16,'blk'=8,'samp'=2] {'blk'}, dimensions={1} | all-to-all | bytes 65536 | tf_op jit(solution)/shard_map/while/body/eval_jaxpr/all_to_all | solution.py:128
  614.0 5.4 collective-permute-done
  619.9 9.2 %all_to_all.15 = f32[8,8,128]{2,0,1:T(8,128)S(1)} all-to-all(f32[8,8,128]{2,0,1:T(8,128)S(1)} %tile.19), channel_id=1, replica_groups=mesh['tm'=16,'blk'=8,'samp'=2] {'blk'}, dimensions={1} | all-to-all | bytes 65536 | tf_op jit(solution)/shard_map/while/body/eval_jaxpr/all_to_all | solution.py:128
  631.1 5.4 collective-permute-done
  637.0 9.2 %all_to_all.15 = f32[8,8,128]{2,0,1:T(8,128)S(1)} all-to-all(f32[8,8,128]{2,0,1:T(8,128)S(1)} %tile.19), channel_id=1, replica_groups=mesh['tm'=16,'blk'=8,'samp'=2] {'blk'}, dimensions={1} | all-to-all | bytes 65536 | tf_op jit(solution)/shard_map/while/body/eval_jaxpr/all_to_all | solution.py:128
  648.2 5.4 collective-permute-done
  654.2 9.2 %all_to_all.15 = f32[8,8,128]{2,0,1:T(8,128)S(1)} all-to-all(f32[8,8,128]{2,0,1:T(8,128)S(1)} %tile.19), channel_id=1, replica_groups=mesh['tm'=16,'blk'=8,'samp'=2] {'blk'}, dimensions={1} | all-to-all | bytes 65536 | tf_op jit(solution)/shard_map/while/body/eval_jaxpr/all_to_all | solution.py:128
  665.3 5.4 collective-permute-done
  671.3 9.2 %all_to_all.15 = f32[8,8,128]{2,0,1:T(8,128)S(1)} all-to-all(f32[8,8,128]{2,0,1:T(8,128)S(1)} %tile.19), channel_id=1, replica_groups=mesh['tm'=16,'blk'=8,'samp'=2] {'blk'}, dimensions={1} | all-to-all | bytes 65536 | tf_op jit(solution)/shard_map/while/body/eval_jaxpr/all_to_all | solution.py:128
  682.4 5.4 collective-permute-done
  688.4 9.2 %all_to_all.15 = f32[8,8,128]{2,0,1:T(8,128)S(1)} all-to-all(f32[8,8,128]{2,0,1:T(8,128)S(1)} %tile.19), channel_id=1, replica_groups=mesh['tm'=16,'blk'=8,'samp'=2] {'blk'}, dimensions={1} | all-to-all | bytes 65536 | tf_op jit(solution)/shard_map/while/body/eval_jaxpr/all_to_all | solution.py:128
  699.6 5.4 collective-permute-done
  705.5 9.2 %all_to_all.15 = f32[8,8,128]{2,0,1:T(8,128)S(1)} all-to-all(f32[8,8,128]{2,0,1:T(8,128)S(1)} %tile.19), channel_id=1, replica_groups=mesh['tm'=16,'blk'=8,'samp'=2] {'blk'}, dimensions={1} | all-to-all | bytes 65536 | tf_op jit(solution)/shard_map/while/body/eval_jaxpr/all_to_all | solution.py:128
  716.7 5.4 collective-permute-done
  722.6 9.2 %all_to_all.15 = f32[8,8,128]{2,0,1:T(8,128)S(1)} all-to-all(f32[8,8,128]{2,0,1:T(8,128)S(1)} %tile.19), channel_id=1, replica_groups=mesh['tm'=16,'blk'=8,'samp'=2] {'blk'}, dimensions={1} | all-to-all | bytes 65536 | tf_op jit(solution)/shard_map/while/body/eval_jaxpr/all_to_all | solution.py:128
  733.8 5.4 collective-permute-done
  739.7 9.2 %all_to_all.15 = f32[8,8,128]{2,0,1:T(8,128)S(1)} all-to-all(f32[8,8,128]{2,0,1:T(8,128)S(1)} %tile.19), channel_id=1, replica_groups=mesh['tm'=16,'blk'=8,'samp'=2] {'blk'}, dimensions={1} | all-to-all | bytes 65536 | tf_op jit(solution)/shard_map/while/body/eval_jaxpr/all_to_all | solution.py:128
  750.9 5.4 collective-permute-done
  756.9 9.2 %all_to_all.15 = f32[8,8,128]{2,0,1:T(8,128)S(1)} all-to-all(f32[8,8,128]{2,0,1:T(8,128)S(1)} %tile.19), channel_id=1, replica_groups=mesh['tm'=16,'blk'=8,'samp'=2] {'blk'}, dimensions={1} | all-to-all | bytes 65536 | tf_op jit(solution)/shard_map/while/body/eval_jaxpr/all_to_all | solution.py:128
  768.0 5.4 collective-permute-done
  (154 shorter events, 56.8 us)
Async XLA Ops:
  6.5 51.7 %all-gather.17.cloned.1.call-start = ((), (), s32[]{:S(2)}) async-start(), calls=%async_computation.5 | async-start | bytes 2359296 | tf_op jit(solution)/shard_map/all_gather | solution.py:80
  16.1 271.2 %copy-start = (bf16[2,128,1024]{2,1,0:T(8,128)(2,1)}, bf16[2,128,1024]{2,1,0:T(8,128)(2,1)S(1)}, u32[]{:S(2)}) copy-start(bf16[2,128,1024]{2,1,0:T(8,128)(2,1)S(1)} %all_gather.56) | copy-start | bytes 1572868
  16.9 144.4 %copy-start.7 = (bf16[2,128,512]{2,1,0:T(8,128)(2,1)S(1)}, bf16[2,128,512]{2,1,0:T(8,128)(2,1)}, u32[]{:S(2)}) copy-start(bf16[2,128,512]{2,1,0:T(8,128)(2,1)} %param.22) | copy-start | bytes 786436
  16.9 123.9 %all-gather.9.cloned.1.call-start = ((), (), s32[]{:S(2)}) async-start(), calls=%async_computation.1 | async-start | bytes 4718592 | tf_op jit(solution)/shard_map/all_gather | solution.py:101
  60.2 13.5 %copy-start.2 = (f32[128,1024]{1,0:T(8,128)}, f32[128,1024]{1,0:T(8,128)S(1)}, u32[]{:S(2)}) copy-start(f32[128,1024]{1,0:T(8,128)S(1)} %fusion.4) | copy-start | bytes 1572868
  60.3 13.5 %collective-permute-start.5 = (f32[128,1024]{1,0:T(8,128)S(1)}, f32[128,1024]{1,0:T(8,128)S(1)}, u32[]{:S(2)}, u32[]{:S(2)}) collective-permute-start(f32[128,1024]{1,0:T(8,128)S(1)} %fusion.4), channel_id=1, source_target_pairs={{0,16},{16,32},{32,48},{48,64},{64,80},{80,96},{96,112},{112,128},... | collective-permute-start | bytes 1572872 | tf_op jit(solution)/shard_map/ppermute | solution.py:25
  73.7 12.6 %collective-permute-start.7 = (f32[128,1024]{1,0:T(8,128)S(1)}, f32[128,1024]{1,0:T(8,128)S(1)}, u32[]{:S(2)}, u32[]{:S(2)}) collective-permute-start(f32[128,1024]{1,0:T(8,128)S(1)} %collective-permute-done.5), channel_id=1, source_target_pairs={{0,16},{16,32},{32,48},{48,64},{64,80},{80,96},{96,112},{112,128},... | collective-permute-start | bytes 1572872 | tf_op jit(solution)/shard_map/ppermute | solution.py:25
  86.3 0.8 copy-start.6
  87.2 128.5 %all-gather.11.cloned.1.call-start = ((), (), s32[]{:S(2)}) async-start(), calls=%async_computation.2 | async-start | bytes 4718592 | tf_op jit(solution)/shard_map/all_gather | solution.py:101
  145.4 91.9 %copy-start.8 = (f32[2,8,32]{2,1,0:T(8,128)S(1)}, f32[2,8,32]{2,1,0:T(8,128)}, u32[]{:S(2)}) copy-start(f32[2,8,32]{2,1,0:T(8,128)} %param.16) | copy-start | bytes 6148
  145.4 94.6 %copy-start.16 = (s32[16]{0:T(128)S(1)}, s32[16]{0:T(128)}, u32[]{:S(2)}) copy-start(s32[16]{0:T(128)} %param.18) | copy-start | bytes 196
  145.4 94.6 %copy-start.9 = (bf16[2,128,128]{2,1,0:T(8,128)(2,1)S(1)}, bf16[2,128,128]{2,1,0:T(8,128)(2,1)}, u32[]{:S(2)}) copy-start(bf16[2,128,128]{2,1,0:T(8,128)(2,1)} %param.21) | copy-start | bytes 196612
  145.5 100.0 %copy-start.10 = (f32[16,8,8]{0,2,1:T(8,128)S(1)}, f32[16,8,8]{0,2,1:T(8,128)}, u32[]{:S(2)}) copy-start(f32[16,8,8]{0,2,1:T(8,128)} %param.17) | copy-start | bytes 12292
  145.5 100.1 %copy-start.11 = (f32[2,8,128]{2,1,0:T(8,128)S(1)}, f32[2,8,128]{2,1,0:T(8,128)}, u32[]{:S(2)}) copy-start(f32[2,8,128]{2,1,0:T(8,128)} %param.13) | copy-start | bytes 24580
  145.5 14.8 %collective-permute-start.9 = (f32[128,1024]{1,0:T(8,128)S(1)}, f32[128,1024]{1,0:T(8,128)S(1)}, u32[]{:S(2)}, u32[]{:S(2)}) collective-permute-start(f32[128,1024]{1,0:T(8,128)S(1)} %fusion.29), channel_id=1, source_target_pairs={{0,32},{16,48},{32,64},{48,80},{64,96},{80,112},{96,128},{112,144}... | collective-permute-start | bytes 1572872 | tf_op jit(solution)/shard_map/ppermute | solution.py:25
  160.3 0.8 copy-start.5
  160.3 85.4 %copy-start.15 = (s32[2,4]{1,0:T(2,128)S(1)}, s32[2,4]{1,0:T(2,128)}, u32[]{:S(2)}) copy-start(s32[2,4]{1,0:T(2,128)} %param.15) | copy-start | bytes 100
  161.2 85.6 %copy-start.14 = (f32[2,32]{1,0:T(2,128)S(1)}, f32[2,32]{1,0:T(2,128)}, u32[]{:S(2)}) copy-start(f32[2,32]{1,0:T(2,128)} %param.14) | copy-start | bytes 772
  161.2 218.6 %all-gather.15.cloned.1.call-start = ((), (), s32[]{:S(2)}) async-start(), calls=%async_computation.4 | async-start | bytes 2359296 | tf_op jit(solution)/shard_map/all_gather | solution.py:85
  170.4 134.7 %copy-start.12 = (f32[8,128]{1,0:T(8,128)S(1)}, f32[8,128]{1,0:T(8,128)}, u32[]{:S(2)}) copy-start(f32[8,128]{1,0:T(8,128)} %param.19) | copy-start | bytes 12292
  170.5 185.3 %copy-start.13 = (f32[4,4]{1,0:T(4,128)S(1)}, f32[4,4]{1,0:T(4,128)}, u32[]{:S(2)}) copy-start(f32[4,4]{1,0:T(4,128)} %param.23) | copy-start | bytes 196
  170.5 229.5 %all-gather.13.cloned.1.call-start = ((), (), s32[]{:S(2)}) async-start(), calls=%async_computation.3 | async-start | bytes 4718592 | tf_op jit(solution)/shard_map/all_gather | solution.py:101
  220.2 16.2 %collective-permute-start.11 = (f32[128,1024]{1,0:T(8,128)S(1)}, f32[128,1024]{1,0:T(8,128)S(1)}, u32[]{:S(2)}, u32[]{:S(2)}) collective-permute-start(f32[128,1024]{1,0:T(8,128)S(1)} %fusion.30), channel_id=1, source_target_pairs={{0,64},{16,80},{32,96},{48,112},{64,128},{80,144},{96,160},{112,17... | collective-permute-start | bytes 1572872 | tf_op jit(solution)/shard_map/ppermute | solution.py:25
  236.4 0.8 copy-start.4
  237.4 8.5 %collective-permute-start.1 = (f32[2,8,16]{2,1,0:T(8,128)S(1)}, f32[2,8,16]{2,1,0:T(8,128)S(1)}, u32[]{:S(2)}, u32[]{:S(2)}) collective-permute-start(f32[2,8,16]{2,1,0:T(8,128)S(1)} %get-tuple-element.108), channel_id=1, source_target_pairs={{0,2},{2,4},{4,6},{6,8},{8,10},{10,12},{12,14},{14,0},{1,3},{3,5},... | collective-permute-start | bytes 3080 | tf_op jit(solution)/shard_map/ppermute | solution.py:16
  237.4 8.5 %collective-permute-start.2 = (f32[2,8,16]{2,1,0:T(8,128)S(1)}, f32[2,8,16]{2,1,0:T(8,128)S(1)}, u32[]{:S(2)}, u32[]{:S(2)}) collective-permute-start(f32[2,8,16]{2,1,0:T(8,128)S(1)} %get-tuple-element.109), channel_id=1, source_target_pairs={{2,0},{4,2},{6,4},{8,6},{10,8},{12,10},{14,12},{0,14},{3,1},{5,3},... | collective-permute-start | bytes 3080 | tf_op jit(solution)/shard_map/ppermute | solution.py:17
  287.5 17.6 %collective-permute-start.3 = (f32[8,128]{1,0:T(8,128)S(1)}, f32[8,128]{1,0:T(8,128)S(1)}, u32[]{:S(2)}, u32[]{:S(2)}) collective-permute-start(f32[8,128]{1,0:T(8,128)S(1)} %convolution_add_fusion.4), channel_id=1, source_target_pairs={{0,16},{16,32},{32,48},{48,64},{64,80},{80,96},{96,112},{112,128},... | collective-permute-start | bytes 12296 | tf_op jit(solution)/shard_map/ppermute | solution.py:25
  305.1 7.0 collective-permute-start.4
  330.6 4.4 collective-permute-start.6
  353.6 5.9 collective-permute-start.8
  378.2 44.9 %copy-start.1 = (bf16[2,128,1024]{2,1,0:T(8,128)(2,1)S(1)}, bf16[2,128,1024]{2,1,0:T(8,128)(2,1)}, u32[]{:S(2)}) copy-start(bf16[2,128,1024]{2,1,0:T(8,128)(2,1)} %copy-done) | copy-start | bytes 1572868
  378.3 45.1 %copy-start.3 = (f32[128,1024]{1,0:T(8,128)S(1)}, f32[128,1024]{1,0:T(8,128)}, u32[]{:S(2)}) copy-start(f32[128,1024]{1,0:T(8,128)} %copy-done.2) | copy-start | bytes 1572868
  378.3 3.5 collective-permute-start.10
  472.4 61.4 %collective-permute-start = (f32[8,1024]{1,0:T(8,128)S(1)}, f32[8,1024]{1,0:T(8,128)S(1)}, u32[]{:S(2)}, u32[]{:S(2)}) collective-permute-start(f32[8,1024]{1,0:T(8,128)S(1)} %bitcast.98), channel_id=1, source_target_pairs={{16,0},{32,16},{48,32},{64,48},{80,64},{96,80},{112,96},{128,112},... | collective-permute-start | bytes 98312 | tf_op jit(solution)/shard_map/while/body/eval_jaxpr/ppermute | solution.py:25
  543.6 7.3 collective-permute-start
  560.7 7.3 collective-permute-start
  577.8 7.3 collective-permute-start
  594.9 7.3 collective-permute-start
  612.0 7.3 collective-permute-start
  629.2 7.3 collective-permute-start
  646.3 7.3 collective-permute-start
  663.4 7.3 collective-permute-start
  680.5 7.3 collective-permute-start
  697.6 7.3 collective-permute-start
  714.8 7.3 collective-permute-start
  731.9 7.3 collective-permute-start
  749.0 7.3 collective-permute-start
  766.1 7.3 collective-permute-start
Sparse Core Ops, SparseCore 0:
  17.0 41.1 all-gather.16
  87.3 53.4 all-gather.8
  161.3 54.2 all-gather.10
  217.3 36.5 all-gather.14
  255.5 56.7 all-gather.12
